TPU v7x, 32 devices: a whole 2x2x4 slice. The times are simulated.
32 devices in a mesh: depth: 8 (over y, x, core), strip: 4 (over z).
Axes of the slice: x: 2, y: 2, z: 4, core: 2. Of those that a mesh axis runs over, the one named last changes fastest.
Arguments:
- arrivals: float32 [8, 1, 4, 128, 128], P('depth', None, None, 'strip'), may hold values from -6 to 6
- feed: float32 [3, 1, 4, 128, 128], P(None, None, None, 'strip'), may hold values from -6 to 6
- velocity_index: int32 [16, 128, 128], P('depth', 'strip'), may hold values from 0 to 31
- offsets: int32 [16], replicated, may hold values from -8 to 8, as said below
- coef_table: float32 [11, 9, 2, 1, 32], replicated, may hold values from -1.8 to 1.8
Outputs:
- image: float32 [16, 16, 128, 128], P('depth', None, 'strip')
- outflow: float32 [8, 1, 4, 128, 128], P('depth', None, None, 'strip')
Inputs may be any that keep to these rules, and one draw needn't show every extreme that they name: The 16 offsets are distinct, and both -8 and 8 occur among them.
All inputs are finite; a program needn't handle non-finite values.
Results may differ from a plain program's by a relative error of at most 0.00025.
Values sent between devices are 32-bit elements; how exact they have to be, the bound alone decides.
No kernel may reach another device: no remote copies, remote signals or barrier semaphores. Data moves between devices by JAX's collectives and lax.ppermute only.
A program may use at most 64 MiB of HBM per device.

v0:
```python
import jax
import jax.numpy as jnp
from jax import lax
from jax.sharding import PartitionSpec as P

LEVELS = 32
ORDER = 8


def with_halo(cells, sides, width):
    for axis, dim in sides:
        count = lax.axis_size(axis)
        ends = count - 1
        head = lax.slice_in_dim(cells, 0, width, axis=dim)
        tail = lax.slice_in_dim(cells, cells.shape[dim] - width, cells.shape[dim], axis=dim)
        cells = jnp.concatenate(
            [
                lax.ppermute(tail, axis, [(i, (i + 1) % count) for i in range(ends)]),
                cells,
                lax.ppermute(head, axis, [((i + 1) % count, i) for i in range(ends)]),
            ],
            axis=dim,
        )
    return cells


def passed_along(value, axis, steps):
    count = lax.axis_size(axis)
    initial, last = (max(0, -steps), min(count, count - steps))
    return lax.ppermute(value, axis, [(source, source + steps) for source in range(initial, last)])


def lateral(field):
    lead = [(0, 0)] * (field.ndim - 2)
    along_y = jnp.pad(field, lead + [(0, 0), (1, 1)])
    smooth_y = field + 0.5 * (along_y[..., 2:] + along_y[..., :-2])
    along_x = jnp.pad(smooth_y, lead + [(1, 1), (0, 0)])
    smooth_x = smooth_y + 0.5 * (along_x[..., 2:, :] + along_x[..., :-2, :])
    return 0.5 * smooth_x - field


def weighted(total, term, coef_re, coef_im):
    source_re = term[..., 0, :, :]
    source_im = term[..., 1, :, :]
    receiver_re = term[..., 2, :, :]
    receiver_im = term[..., 3, :, :]
    piece = jnp.stack(
        [
            coef_re * source_re - coef_im * source_im,
            coef_re * source_im + coef_im * source_re,
            coef_re * receiver_re + coef_im * receiver_im,
            coef_re * receiver_im - coef_im * receiver_re,
        ],
        axis=-3,
    )
    return total + piece


def edge_mask(strip_pos, width, total_cells, margin):
    cells = strip_pos * width - margin + jnp.arange(width + 2 * margin, dtype=jnp.int32)
    return ((cells >= 0) & (cells < total_cells)).astype(jnp.float32)[:, None]


def level_hot(levels):
    flattened = levels.reshape(1, -1)
    return (jnp.arange(LEVELS, dtype=jnp.int32).reshape(-1, 1) == flattened).astype(jnp.float32)


def coef_sets(batch_table, hot, span, lane_cells):
    flattened = jnp.dot(
        batch_table.reshape(-1, batch_table.shape[-1]),
        hot,
        precision=lax.Precision.HIGHEST,
        preferred_element_type=jnp.float32,
    )
    return flattened.reshape(batch_table.shape[0], 2, batch_table.shape[2], span, lane_cells)


def extrapolate(padded, coefficients, mask, start, count):

    def kept(values):
        return lax.slice_in_dim(values, start, start + count, axis=2)

    earlier = padded
    total = weighted(
        jnp.zeros_like(kept(padded)), kept(padded), coefficients[0, 0], coefficients[0, 1]
    )
    current = lateral(padded) * mask
    total = weighted(total, kept(current), coefficients[1, 0], coefficients[1, 1])
    for order in range(2, ORDER + 1):
        following = (2.0 * lateral(current) - earlier) * mask
        earlier, current = (current, following)
        total = weighted(total, kept(current), coefficients[order, 0], coefficients[order, 1])
    return total


def offset_image(padded, margin, offsets, width):
    rows = []
    for index in range(offsets.shape[0]):
        offset = offsets[index]
        source = lax.dynamic_slice_in_dim(padded, margin - offset, width, axis=2)
        receiver = lax.dynamic_slice_in_dim(padded, margin + offset, width, axis=2)
        rows.append(jnp.sum(source[:, 0] * receiver[:, 2] + source[:, 1] * receiver[:, 3], axis=0))
    return jnp.stack(rows, axis=0)


def per_device(arrivals, feed, velocity_index, offsets, coef_table):
    field = arrivals[0]
    width = field.shape[2]
    lane_cells = field.shape[3]
    section = lax.axis_index("depth")
    sections = lax.axis_size("depth")
    strip_pos = lax.axis_index("strip")
    total_cells = width * lax.axis_size("strip")
    layers = velocity_index.shape[0]
    ticks = feed.shape[0] + 1
    image = jnp.zeros((layers, offsets.shape[0], width, lane_cells), jnp.float32)
    level_hots = [level_hot(velocity_index[row]) for row in range(layers)]
    mask = edge_mask(strip_pos, width, total_cells, ORDER)
    for tick in range(ticks):
        batch_table = lax.dynamic_index_in_dim(
            coef_table, tick - section + sections - 1, 0, keepdims=False
        )
        for row in range(layers):
            padded = with_halo(field, (("strip", 2),), ORDER)
            if row > 0:
                image = image.at[row - 1].add(offset_image(padded, ORDER, offsets, width))
            coefficients = coef_sets(batch_table, level_hots[row], width, lane_cells)
            field = extrapolate(padded, coefficients, mask, ORDER, width)
        padded = with_halo(field, (("strip", 2),), ORDER)
        image = image.at[layers - 1].add(offset_image(padded, ORDER, offsets, width))
        if tick + 1 < ticks:
            moved = passed_along(field, "depth", 1)
            field = jnp.where(section == 0, feed[tick], moved)
    return (image, field[None])


def solution(mesh):
    placed = (
        P("depth", None, None, "strip", None),
        P(None, None, None, "strip", None),
        P("depth", "strip", None),
        P(),
        P(),
    )
    return jax.shard_map(
        per_device,
        mesh=mesh,
        in_specs=placed,
        out_specs=(P("depth", None, "strip", None), P("depth", None, None, "strip", None)),
        check_vma=False,
    )
```

profile of v0, /device:TPU:28, one launch (start us, length us, event | category | flops | bytes accessed | tf_op | source)
XLA Modules:
  0.0 177.2 jit_solution(9128985686359997652)
XLA Ops:
  2.0 2.3 %collective-permute-start.1 = (f32[1,4,8,128]{3,2,1,0:T(8,128)}, f32[1,4,8,128]{3,2,1,0:T(8,128)S(1)}, u32[]{:S(2)}, u32[]{:S(2)}) collective-permute-start(f32[1,4,8,128]{3,2,1,0:T(8,128)} %get-tuple-element.463), channel_id=1, source_target_pairs={{1,0},{2,1},{3,2},{5,4},{6,5},{7,6},{9,8},{10,9},{11,10},{13,12},{... | collective-permute-start | bytes 49160 | tf_op jit(solution)/shard_map/ppermute | solution.py:20
  65.8 4.7 %collective-permute-start.3 = (f32[1,4,8,128]{3,2,1,0:T(8,128)S(1)}, f32[1,4,8,128]{3,2,1,0:T(8,128)S(1)}, u32[]{:S(2)}, u32[]{:S(2)}) collective-permute-start(f32[1,4,8,128]{3,2,1,0:T(8,128)S(1)} %get-tuple-element.461), channel_id=1, source_target_pairs={{1,0},{2,1},{3,2},{5,4},{6,5},{7,6},{9,8},{10,9},{11,10},{13,12},{... | collective-permute-start | bytes 49160 | tf_op jit(solution)/shard_map/ppermute | solution.py:20
  71.9 4.2 %collective-permute-done.2 = f32[1,4,8,128]{3,2,1,0:T(8,128)S(1)} collective-permute-done((f32[1,4,8,128]{3,2,1,0:T(8,128)S(1)}, f32[1,4,8,128]{3,2,1,0:T(8,128)S(1)}, u32[]{:S(2)}, u32[]{:S(2)}) %collective-permute-start.2) | collective-permute-done | bytes 16416 | tf_op jit(solution)/shard_map/ppermute | solution.py:18
  77.9 1.9 %collective-permute-start.6 = (f32[1,4,32,128]{3,2,1,0:T(8,128)S(1)}, f32[1,4,32,128]{3,2,1,0:T(8,128)S(1)}, u32[]{:S(2)}, u32[]{:S(2)}) collective-permute-start(f32[1,4,32,128]{3,2,1,0:T(8,128)S(1)} %fusion.723), channel_id=1, source_target_pairs={{0,4},{4,8},{8,12},{12,16},{16,20},{20,24},{24,28},{1,5},{5,9},{9,... | collective-permute-start | bytes 196616 | tf_op jit(solution)/shard_map/ppermute | solution.py:30
  79.8 2.4 %collective-permute-start.5 = (f32[1,4,8,128]{3,2,1,0:T(8,128)S(1)}, f32[1,4,8,128]{3,2,1,0:T(8,128)S(1)}, u32[]{:S(2)}, u32[]{:S(2)}) collective-permute-start(f32[1,4,8,128]{3,2,1,0:T(8,128)S(1)} %get-tuple-element.459), channel_id=1, source_target_pairs={{1,0},{2,1},{3,2},{5,4},{6,5},{7,6},{9,8},{10,9},{11,10},{13,12},{... | collective-permute-start | bytes 49160 | tf_op jit(solution)/shard_map/ppermute | solution.py:20
  84.3 3.6 %collective-permute-done.4 = f32[1,4,8,128]{3,2,1,0:T(8,128)S(1)} collective-permute-done((f32[1,4,8,128]{3,2,1,0:T(8,128)S(1)}, f32[1,4,8,128]{3,2,1,0:T(8,128)S(1)}, u32[]{:S(2)}, u32[]{:S(2)}) %collective-permute-start.4) | collective-permute-done | bytes 16416 | tf_op jit(solution)/shard_map/ppermute | solution.py:18
  89.4 2.4 %collective-permute-start.8 = (f32[1,4,8,128]{3,2,1,0:T(8,128)S(1)}, f32[1,4,8,128]{3,2,1,0:T(8,128)S(1)}, u32[]{:S(2)}, u32[]{:S(2)}) collective-permute-start(f32[1,4,8,128]{3,2,1,0:T(8,128)S(1)} %get-tuple-element.457), channel_id=1, source_target_pairs={{1,0},{2,1},{3,2},{5,4},{6,5},{7,6},{9,8},{10,9},{11,10},{13,12},{... | collective-permute-start | bytes 49160 | tf_op jit(solution)/shard_map/ppermute | solution.py:20
  93.2 4.2 %collective-permute-done.7 = f32[1,4,8,128]{3,2,1,0:T(8,128)S(1)} collective-permute-done((f32[1,4,8,128]{3,2,1,0:T(8,128)S(1)}, f32[1,4,8,128]{3,2,1,0:T(8,128)S(1)}, u32[]{:S(2)}, u32[]{:S(2)}) %collective-permute-start.7) | collective-permute-done | bytes 16416 | tf_op jit(solution)/shard_map/ppermute | solution.py:18
  99.2 1.9 %collective-permute-start.10 = (f32[1,4,8,128]{3,2,1,0:T(8,128)S(1)}, f32[1,4,8,128]{3,2,1,0:T(8,128)S(1)}, u32[]{:S(2)}, u32[]{:S(2)}) collective-permute-start(f32[1,4,8,128]{3,2,1,0:T(8,128)S(1)} %get-tuple-element.455), channel_id=1, source_target_pairs={{1,0},{2,1},{3,2},{5,4},{6,5},{7,6},{9,8},{10,9},{11,10},{13,12},{... | collective-permute-start | bytes 49160 | tf_op jit(solution)/shard_map/ppermute | solution.py:20
  102.6 4.2 %collective-permute-done.9 = f32[1,4,8,128]{3,2,1,0:T(8,128)S(1)} collective-permute-done((f32[1,4,8,128]{3,2,1,0:T(8,128)S(1)}, f32[1,4,8,128]{3,2,1,0:T(8,128)S(1)}, u32[]{:S(2)}, u32[]{:S(2)}) %collective-permute-start.9) | collective-permute-done | bytes 16416 | tf_op jit(solution)/shard_map/ppermute | solution.py:18
  108.6 1.9 %collective-permute-start.13 = (f32[1,4,32,128]{3,2,1,0:T(8,128)S(1)}, f32[1,4,32,128]{3,2,1,0:T(8,128)S(1)}, u32[]{:S(2)}, u32[]{:S(2)}) collective-permute-start(f32[1,4,32,128]{3,2,1,0:T(8,128)S(1)} %fusion.737), channel_id=1, source_target_pairs={{0,4},{4,8},{8,12},{12,16},{16,20},{20,24},{24,28},{1,5},{5,9},{9,... | collective-permute-start | bytes 196616 | tf_op jit(solution)/shard_map/ppermute | solution.py:30
  111.1 1.9 %collective-permute-start.12 = (f32[1,4,8,128]{3,2,1,0:T(8,128)S(1)}, f32[1,4,8,128]{3,2,1,0:T(8,128)S(1)}, u32[]{:S(2)}, u32[]{:S(2)}) collective-permute-start(f32[1,4,8,128]{3,2,1,0:T(8,128)S(1)} %get-tuple-element.453), channel_id=1, source_target_pairs={{1,0},{2,1},{3,2},{5,4},{6,5},{7,6},{9,8},{10,9},{11,10},{13,12},{... | collective-permute-start | bytes 49160 | tf_op jit(solution)/shard_map/ppermute | solution.py:20
  114.6 4.1 %collective-permute-done.11 = f32[1,4,8,128]{3,2,1,0:T(8,128)S(1)} collective-permute-done((f32[1,4,8,128]{3,2,1,0:T(8,128)S(1)}, f32[1,4,8,128]{3,2,1,0:T(8,128)S(1)}, u32[]{:S(2)}, u32[]{:S(2)}) %collective-permute-start.11) | collective-permute-done | bytes 16416 | tf_op jit(solution)/shard_map/ppermute | solution.py:18
  119.3 1.9 %collective-permute-start.15 = (f32[1,4,8,128]{3,2,1,0:T(8,128)S(1)}, f32[1,4,8,128]{3,2,1,0:T(8,128)S(1)}, u32[]{:S(2)}, u32[]{:S(2)}) collective-permute-start(f32[1,4,8,128]{3,2,1,0:T(8,128)S(1)} %get-tuple-element.451), channel_id=1, source_target_pairs={{1,0},{2,1},{3,2},{5,4},{6,5},{7,6},{9,8},{10,9},{11,10},{13,12},{... | collective-permute-start | bytes 49160 | tf_op jit(solution)/shard_map/ppermute | solution.py:20
  122.7 4.2 %collective-permute-done.14 = f32[1,4,8,128]{3,2,1,0:T(8,128)S(1)} collective-permute-done((f32[1,4,8,128]{3,2,1,0:T(8,128)S(1)}, f32[1,4,8,128]{3,2,1,0:T(8,128)S(1)}, u32[]{:S(2)}, u32[]{:S(2)}) %collective-permute-start.14) | collective-permute-done | bytes 16416 | tf_op jit(solution)/shard_map/ppermute | solution.py:18
  128.7 1.9 %collective-permute-start.17 = (f32[1,4,8,128]{3,2,1,0:T(8,128)S(1)}, f32[1,4,8,128]{3,2,1,0:T(8,128)S(1)}, u32[]{:S(2)}, u32[]{:S(2)}) collective-permute-start(f32[1,4,8,128]{3,2,1,0:T(8,128)S(1)} %get-tuple-element.449), channel_id=1, source_target_pairs={{1,0},{2,1},{3,2},{5,4},{6,5},{7,6},{9,8},{10,9},{11,10},{13,12},{... | collective-permute-start | bytes 49160 | tf_op jit(solution)/shard_map/ppermute | solution.py:20
  132.1 4.2 %collective-permute-done.16 = f32[1,4,8,128]{3,2,1,0:T(8,128)S(1)} collective-permute-done((f32[1,4,8,128]{3,2,1,0:T(8,128)S(1)}, f32[1,4,8,128]{3,2,1,0:T(8,128)S(1)}, u32[]{:S(2)}, u32[]{:S(2)}) %collective-permute-start.16) | collective-permute-done | bytes 16416 | tf_op jit(solution)/shard_map/ppermute | solution.py:18
  138.2 1.9 %collective-permute-start.20 = (f32[1,4,32,128]{3,2,1,0:T(8,128)S(1)}, f32[1,4,32,128]{3,2,1,0:T(8,128)S(1)}, u32[]{:S(2)}, u32[]{:S(2)}) collective-permute-start(f32[1,4,32,128]{3,2,1,0:T(8,128)S(1)} %fusion.751), channel_id=1, source_target_pairs={{0,4},{4,8},{8,12},{12,16},{16,20},{20,24},{24,28},{1,5},{5,9},{9,... | collective-permute-start | bytes 196616 | tf_op jit(solution)/shard_map/ppermute | solution.py:30
  140.6 1.9 %collective-permute-start.19 = (f32[1,4,8,128]{3,2,1,0:T(8,128)S(1)}, f32[1,4,8,128]{3,2,1,0:T(8,128)S(1)}, u32[]{:S(2)}, u32[]{:S(2)}) collective-permute-start(f32[1,4,8,128]{3,2,1,0:T(8,128)S(1)} %get-tuple-element.447), channel_id=1, source_target_pairs={{1,0},{2,1},{3,2},{5,4},{6,5},{7,6},{9,8},{10,9},{11,10},{13,12},{... | collective-permute-start | bytes 49160 | tf_op jit(solution)/shard_map/ppermute | solution.py:20
  144.0 4.2 %collective-permute-done.18 = f32[1,4,8,128]{3,2,1,0:T(8,128)S(1)} collective-permute-done((f32[1,4,8,128]{3,2,1,0:T(8,128)S(1)}, f32[1,4,8,128]{3,2,1,0:T(8,128)S(1)}, u32[]{:S(2)}, u32[]{:S(2)}) %collective-permute-start.18) | collective-permute-done | bytes 16416 | tf_op jit(solution)/shard_map/ppermute | solution.py:18
  152.2 4.2 %collective-permute-done.21 = f32[1,4,8,128]{3,2,1,0:T(8,128)S(1)} collective-permute-done((f32[1,4,8,128]{3,2,1,0:T(8,128)S(1)}, f32[1,4,8,128]{3,2,1,0:T(8,128)S(1)}, u32[]{:S(2)}, u32[]{:S(2)}) %collective-permute-start.21) | collective-permute-done | bytes 16416 | tf_op jit(solution)/shard_map/ppermute | solution.py:18
  161.6 4.2 %collective-permute-done.23 = f32[1,4,8,128]{3,2,1,0:T(8,128)S(1)} collective-permute-done((f32[1,4,8,128]{3,2,1,0:T(8,128)S(1)}, f32[1,4,8,128]{3,2,1,0:T(8,128)S(1)}, u32[]{:S(2)}, u32[]{:S(2)}) %collective-permute-start.23) | collective-permute-done | bytes 16416 | tf_op jit(solution)/shard_map/ppermute | solution.py:18
  168.2 1.9 %collective-permute-start.26 = (f32[1,4,8,128]{3,2,1,0:T(8,128)S(1)}, f32[1,4,8,128]{3,2,1,0:T(8,128)S(1)}, u32[]{:S(2)}, u32[]{:S(2)}) collective-permute-start(f32[1,4,8,128]{3,2,1,0:T(8,128)S(1)} %get-tuple-element.441), channel_id=1, source_target_pairs={{1,0},{2,1},{3,2},{5,4},{6,5},{7,6},{9,8},{10,9},{11,10},{13,12},{... | collective-permute-start | bytes 49160 | tf_op jit(solution)/shard_map/ppermute | solution.py:20
  172.3 3.5 %collective-permute-done.25 = f32[1,4,8,128]{3,2,1,0:T(8,128)S(1)} collective-permute-done((f32[1,4,8,128]{3,2,1,0:T(8,128)S(1)}, f32[1,4,8,128]{3,2,1,0:T(8,128)S(1)}, u32[]{:S(2)}, u32[]{:S(2)}) %collective-permute-start.25) | collective-permute-done | bytes 16416 | tf_op jit(solution)/shard_map/ppermute | solution.py:18
  (494 shorter events, 59.8 us)
Async XLA Ops:
  2.0 55.5 %collective-permute-start.1 = (f32[1,4,8,128]{3,2,1,0:T(8,128)}, f32[1,4,8,128]{3,2,1,0:T(8,128)S(1)}, u32[]{:S(2)}, u32[]{:S(2)}) collective-permute-start(f32[1,4,8,128]{3,2,1,0:T(8,128)} %get-tuple-element.463), channel_id=1, source_target_pairs={{1,0},{2,1},{3,2},{5,4},{6,5},{7,6},{9,8},{10,9},{11,10},{13,12},{... | collective-permute-start | bytes 49160 | tf_op jit(solution)/shard_map/ppermute | solution.py:20
  4.3 53.2 %collective-permute-start = (f32[1,4,8,128]{3,2,1,0:T(8,128)}, f32[1,4,8,128]{3,2,1,0:T(8,128)S(1)}, u32[]{:S(2)}, u32[]{:S(2)}) collective-permute-start(f32[1,4,8,128]{3,2,1,0:T(8,128)} %get-tuple-element.462), channel_id=1, source_target_pairs={{0,1},{1,2},{2,3},{4,5},{5,6},{6,7},{8,9},{9,10},{10,11},{12,13},{... | collective-permute-start | bytes 49160 | tf_op jit(solution)/shard_map/ppermute | solution.py:18
  65.8 6.1 %collective-permute-start.3 = (f32[1,4,8,128]{3,2,1,0:T(8,128)S(1)}, f32[1,4,8,128]{3,2,1,0:T(8,128)S(1)}, u32[]{:S(2)}, u32[]{:S(2)}) collective-permute-start(f32[1,4,8,128]{3,2,1,0:T(8,128)S(1)} %get-tuple-element.461), channel_id=1, source_target_pairs={{1,0},{2,1},{3,2},{5,4},{6,5},{7,6},{9,8},{10,9},{11,10},{13,12},{... | collective-permute-start | bytes 49160 | tf_op jit(solution)/shard_map/ppermute | solution.py:20
  70.4 5.6 %collective-permute-start.2 = (f32[1,4,8,128]{3,2,1,0:T(8,128)S(1)}, f32[1,4,8,128]{3,2,1,0:T(8,128)S(1)}, u32[]{:S(2)}, u32[]{:S(2)}) collective-permute-start(f32[1,4,8,128]{3,2,1,0:T(8,128)S(1)} %get-tuple-element.460), channel_id=1, source_target_pairs={{0,1},{1,2},{2,3},{4,5},{5,6},{6,7},{8,9},{9,10},{10,11},{12,13},{... | collective-permute-start | bytes 49160 | tf_op jit(solution)/shard_map/ppermute | solution.py:18
  77.9 10.6 %collective-permute-start.6 = (f32[1,4,32,128]{3,2,1,0:T(8,128)S(1)}, f32[1,4,32,128]{3,2,1,0:T(8,128)S(1)}, u32[]{:S(2)}, u32[]{:S(2)}) collective-permute-start(f32[1,4,32,128]{3,2,1,0:T(8,128)S(1)} %fusion.723), channel_id=1, source_target_pairs={{0,4},{4,8},{8,12},{12,16},{16,20},{20,24},{24,28},{1,5},{5,9},{9,... | collective-permute-start | bytes 196616 | tf_op jit(solution)/shard_map/ppermute | solution.py:30
  79.8 4.4 %collective-permute-start.5 = (f32[1,4,8,128]{3,2,1,0:T(8,128)S(1)}, f32[1,4,8,128]{3,2,1,0:T(8,128)S(1)}, u32[]{:S(2)}, u32[]{:S(2)}) collective-permute-start(f32[1,4,8,128]{3,2,1,0:T(8,128)S(1)} %get-tuple-element.459), channel_id=1, source_target_pairs={{1,0},{2,1},{3,2},{5,4},{6,5},{7,6},{9,8},{10,9},{11,10},{13,12},{... | collective-permute-start | bytes 49160 | tf_op jit(solution)/shard_map/ppermute | solution.py:20
  82.2 5.6 %collective-permute-start.4 = (f32[1,4,8,128]{3,2,1,0:T(8,128)S(1)}, f32[1,4,8,128]{3,2,1,0:T(8,128)S(1)}, u32[]{:S(2)}, u32[]{:S(2)}) collective-permute-start(f32[1,4,8,128]{3,2,1,0:T(8,128)S(1)} %get-tuple-element.458), channel_id=1, source_target_pairs={{0,1},{1,2},{2,3},{4,5},{5,6},{6,7},{8,9},{9,10},{10,11},{12,13},{... | collective-permute-start | bytes 49160 | tf_op jit(solution)/shard_map/ppermute | solution.py:18
  89.4 3.8 %collective-permute-start.8 = (f32[1,4,8,128]{3,2,1,0:T(8,128)S(1)}, f32[1,4,8,128]{3,2,1,0:T(8,128)S(1)}, u32[]{:S(2)}, u32[]{:S(2)}) collective-permute-start(f32[1,4,8,128]{3,2,1,0:T(8,128)S(1)} %get-tuple-element.457), channel_id=1, source_target_pairs={{1,0},{2,1},{3,2},{5,4},{6,5},{7,6},{9,8},{10,9},{11,10},{13,12},{... | collective-permute-start | bytes 49160 | tf_op jit(solution)/shard_map/ppermute | solution.py:20
  91.7 5.6 %collective-permute-start.7 = (f32[1,4,8,128]{3,2,1,0:T(8,128)S(1)}, f32[1,4,8,128]{3,2,1,0:T(8,128)S(1)}, u32[]{:S(2)}, u32[]{:S(2)}) collective-permute-start(f32[1,4,8,128]{3,2,1,0:T(8,128)S(1)} %get-tuple-element.456), channel_id=1, source_target_pairs={{0,1},{1,2},{2,3},{4,5},{5,6},{6,7},{8,9},{9,10},{10,11},{12,13},{... | collective-permute-start | bytes 49160 | tf_op jit(solution)/shard_map/ppermute | solution.py:18
  99.2 3.4 %collective-permute-start.10 = (f32[1,4,8,128]{3,2,1,0:T(8,128)S(1)}, f32[1,4,8,128]{3,2,1,0:T(8,128)S(1)}, u32[]{:S(2)}, u32[]{:S(2)}) collective-permute-start(f32[1,4,8,128]{3,2,1,0:T(8,128)S(1)} %get-tuple-element.455), channel_id=1, source_target_pairs={{1,0},{2,1},{3,2},{5,4},{6,5},{7,6},{9,8},{10,9},{11,10},{13,12},{... | collective-permute-start | bytes 49160 | tf_op jit(solution)/shard_map/ppermute | solution.py:20
  101.1 5.6 %collective-permute-start.9 = (f32[1,4,8,128]{3,2,1,0:T(8,128)S(1)}, f32[1,4,8,128]{3,2,1,0:T(8,128)S(1)}, u32[]{:S(2)}, u32[]{:S(2)}) collective-permute-start(f32[1,4,8,128]{3,2,1,0:T(8,128)S(1)} %get-tuple-element.454), channel_id=1, source_target_pairs={{0,1},{1,2},{2,3},{4,5},{5,6},{6,7},{8,9},{9,10},{10,11},{12,13},{... | collective-permute-start | bytes 49160 | tf_op jit(solution)/shard_map/ppermute | solution.py:18
  108.6 10.7 %collective-permute-start.13 = (f32[1,4,32,128]{3,2,1,0:T(8,128)S(1)}, f32[1,4,32,128]{3,2,1,0:T(8,128)S(1)}, u32[]{:S(2)}, u32[]{:S(2)}) collective-permute-start(f32[1,4,32,128]{3,2,1,0:T(8,128)S(1)} %fusion.737), channel_id=1, source_target_pairs={{0,4},{4,8},{8,12},{12,16},{16,20},{20,24},{24,28},{1,5},{5,9},{9,... | collective-permute-start | bytes 196616 | tf_op jit(solution)/shard_map/ppermute | solution.py:30
  111.1 3.5 %collective-permute-start.12 = (f32[1,4,8,128]{3,2,1,0:T(8,128)S(1)}, f32[1,4,8,128]{3,2,1,0:T(8,128)S(1)}, u32[]{:S(2)}, u32[]{:S(2)}) collective-permute-start(f32[1,4,8,128]{3,2,1,0:T(8,128)S(1)} %get-tuple-element.453), channel_id=1, source_target_pairs={{1,0},{2,1},{3,2},{5,4},{6,5},{7,6},{9,8},{10,9},{11,10},{13,12},{... | collective-permute-start | bytes 49160 | tf_op jit(solution)/shard_map/ppermute | solution.py:20
  113.0 5.6 %collective-permute-start.11 = (f32[1,4,8,128]{3,2,1,0:T(8,128)S(1)}, f32[1,4,8,128]{3,2,1,0:T(8,128)S(1)}, u32[]{:S(2)}, u32[]{:S(2)}) collective-permute-start(f32[1,4,8,128]{3,2,1,0:T(8,128)S(1)} %get-tuple-element.452), channel_id=1, source_target_pairs={{0,1},{1,2},{2,3},{4,5},{5,6},{6,7},{8,9},{9,10},{10,11},{12,13},{... | collective-permute-start | bytes 49160 | tf_op jit(solution)/shard_map/ppermute | solution.py:18
  119.3 3.4 %collective-permute-start.15 = (f32[1,4,8,128]{3,2,1,0:T(8,128)S(1)}, f32[1,4,8,128]{3,2,1,0:T(8,128)S(1)}, u32[]{:S(2)}, u32[]{:S(2)}) collective-permute-start(f32[1,4,8,128]{3,2,1,0:T(8,128)S(1)} %get-tuple-element.451), channel_id=1, source_target_pairs={{1,0},{2,1},{3,2},{5,4},{6,5},{7,6},{9,8},{10,9},{11,10},{13,12},{... | collective-permute-start | bytes 49160 | tf_op jit(solution)/shard_map/ppermute | solution.py:20
  121.3 5.6 %collective-permute-start.14 = (f32[1,4,8,128]{3,2,1,0:T(8,128)S(1)}, f32[1,4,8,128]{3,2,1,0:T(8,128)S(1)}, u32[]{:S(2)}, u32[]{:S(2)}) collective-permute-start(f32[1,4,8,128]{3,2,1,0:T(8,128)S(1)} %get-tuple-element.450), channel_id=1, source_target_pairs={{0,1},{1,2},{2,3},{4,5},{5,6},{6,7},{8,9},{9,10},{10,11},{12,13},{... | collective-permute-start | bytes 49160 | tf_op jit(solution)/shard_map/ppermute | solution.py:18
  128.7 3.4 %collective-permute-start.17 = (f32[1,4,8,128]{3,2,1,0:T(8,128)S(1)}, f32[1,4,8,128]{3,2,1,0:T(8,128)S(1)}, u32[]{:S(2)}, u32[]{:S(2)}) collective-permute-start(f32[1,4,8,128]{3,2,1,0:T(8,128)S(1)} %get-tuple-element.449), channel_id=1, source_target_pairs={{1,0},{2,1},{3,2},{5,4},{6,5},{7,6},{9,8},{10,9},{11,10},{13,12},{... | collective-permute-start | bytes 49160 | tf_op jit(solution)/shard_map/ppermute | solution.py:20
  130.7 5.6 %collective-permute-start.16 = (f32[1,4,8,128]{3,2,1,0:T(8,128)S(1)}, f32[1,4,8,128]{3,2,1,0:T(8,128)S(1)}, u32[]{:S(2)}, u32[]{:S(2)}) collective-permute-start(f32[1,4,8,128]{3,2,1,0:T(8,128)S(1)} %get-tuple-element.448), channel_id=1, source_target_pairs={{0,1},{1,2},{2,3},{4,5},{5,6},{6,7},{8,9},{9,10},{10,11},{12,13},{... | collective-permute-start | bytes 49160 | tf_op jit(solution)/shard_map/ppermute | solution.py:18
  138.2 10.7 %collective-permute-start.20 = (f32[1,4,32,128]{3,2,1,0:T(8,128)S(1)}, f32[1,4,32,128]{3,2,1,0:T(8,128)S(1)}, u32[]{:S(2)}, u32[]{:S(2)}) collective-permute-start(f32[1,4,32,128]{3,2,1,0:T(8,128)S(1)} %fusion.751), channel_id=1, source_target_pairs={{0,4},{4,8},{8,12},{12,16},{16,20},{20,24},{24,28},{1,5},{5,9},{9,... | collective-permute-start | bytes 196616 | tf_op jit(solution)/shard_map/ppermute | solution.py:30
  142.5 5.6 %collective-permute-start.18 = (f32[1,4,8,128]{3,2,1,0:T(8,128)S(1)}, f32[1,4,8,128]{3,2,1,0:T(8,128)S(1)}, u32[]{:S(2)}, u32[]{:S(2)}) collective-permute-start(f32[1,4,8,128]{3,2,1,0:T(8,128)S(1)} %get-tuple-element.446), channel_id=1, source_target_pairs={{0,1},{1,2},{2,3},{4,5},{5,6},{6,7},{8,9},{9,10},{10,11},{12,13},{... | collective-permute-start | bytes 49160 | tf_op jit(solution)/shard_map/ppermute | solution.py:18
  150.8 5.6 %collective-permute-start.21 = (f32[1,4,8,128]{3,2,1,0:T(8,128)S(1)}, f32[1,4,8,128]{3,2,1,0:T(8,128)S(1)}, u32[]{:S(2)}, u32[]{:S(2)}) collective-permute-start(f32[1,4,8,128]{3,2,1,0:T(8,128)S(1)} %get-tuple-element.444), channel_id=1, source_target_pairs={{0,1},{1,2},{2,3},{4,5},{5,6},{6,7},{8,9},{9,10},{10,11},{12,13},{... | collective-permute-start | bytes 49160 | tf_op jit(solution)/shard_map/ppermute | solution.py:18
  160.2 5.6 %collective-permute-start.23 = (f32[1,4,8,128]{3,2,1,0:T(8,128)S(1)}, f32[1,4,8,128]{3,2,1,0:T(8,128)S(1)}, u32[]{:S(2)}, u32[]{:S(2)}) collective-permute-start(f32[1,4,8,128]{3,2,1,0:T(8,128)S(1)} %get-tuple-element.442), channel_id=1, source_target_pairs={{0,1},{1,2},{2,3},{4,5},{5,6},{6,7},{8,9},{9,10},{10,11},{12,13},{... | collective-permute-start | bytes 49160 | tf_op jit(solution)/shard_map/ppermute | solution.py:18
  168.2 4.1 %collective-permute-start.26 = (f32[1,4,8,128]{3,2,1,0:T(8,128)S(1)}, f32[1,4,8,128]{3,2,1,0:T(8,128)S(1)}, u32[]{:S(2)}, u32[]{:S(2)}) collective-permute-start(f32[1,4,8,128]{3,2,1,0:T(8,128)S(1)} %get-tuple-element.441), channel_id=1, source_target_pairs={{1,0},{2,1},{3,2},{5,4},{6,5},{7,6},{9,8},{10,9},{11,10},{13,12},{... | collective-permute-start | bytes 49160 | tf_op jit(solution)/shard_map/ppermute | solution.py:20
  170.2 5.6 %collective-permute-start.25 = (f32[1,4,8,128]{3,2,1,0:T(8,128)S(1)}, f32[1,4,8,128]{3,2,1,0:T(8,128)S(1)}, u32[]{:S(2)}, u32[]{:S(2)}) collective-permute-start(f32[1,4,8,128]{3,2,1,0:T(8,128)S(1)} %get-tuple-element.440), channel_id=1, source_target_pairs={{0,1},{1,2},{2,3},{4,5},{5,6},{6,7},{8,9},{9,10},{10,11},{12,13},{... | collective-permute-start | bytes 49160 | tf_op jit(solution)/shard_map/ppermute | solution.py:18
  (31 other events, 48.2 us)
where the time goes:
time: 180 us; the launch traced here: 177 us
  starting transfers between devices  48.5 us (27%)
  waiting for transfers between devices  45.6 us (25%)
  between operations  43.6 us (24%)
  other arithmetic  19.5 us (11%)
  local copies, waits for them, and re-layouts  16.4 us (9%)
  matrix products  3.63 us (2%)
    ppermute x12, waiting for transfers between devices, with_halo(): lax.ppermute(tail, axis, [(i, (i + 1) % count) for i in range(ends)])  44.8 us
    ppermute x12, starting transfers between devices, with_halo(): lax.ppermute(head, axis, [((i + 1) % count, i) for i in range(ends)])  27.1 us
    ppermute x12, starting transfers between devices, with_halo(): lax.ppermute(tail, axis, [(i, (i + 1) % count) for i in range(ends)])  15.7 us
    unnamed x71, local copies, waits for them, and re-layouts  8.78 us
    add x64, other arithmetic, lateral(): smooth_y = field + 0.5 * (along_y[..., 2:] + along_y[..., :-2])  7.42 us
    ppermute x3, starting transfers between devices, passed_along(): lax.ppermute(value, axis, [(source, source + steps) for source in range(i...  5.76 us
    mul x56, other arithmetic, extrapolate(): following = (2.0 * lateral(current) - earlier) * mask  4.38 us
    dot_general x7, local copies, waits for them, and re-layouts, coef_sets(): jnp.dot(batch_table.reshape(-1, batch_table.shape[-1]), hot, precision=la...  3.89 us
  transfers between devices with their start and end apart: 27, of which 18 were waited for; matrix products, arithmetic and copies ran while one was open for 8% of the time, Pallas kernels for 0%

commit v1 on v0

v1 whole, which is shorter than its diff:
```python
import functools

import jax
import jax.numpy as jnp
from jax import lax
from jax.experimental import pallas as pl
from jax.experimental.pallas import tpu as pltpu
from jax.sharding import PartitionSpec as P

SUB = 8
LANES = 128
VMEM = pl.BlockSpec(memory_space=pltpu.VMEM)
SMEM = pl.BlockSpec(memory_space=pltpu.SMEM)


def layer_step(terms, smooth, table_ref, table_row, velocity_ref, layer, start, rows, orders, wides, left, right):
    tiles = rows // SUB
    comps = terms.shape[1]
    zero = jnp.zeros((SUB, LANES), jnp.float32)
    base = pl.multiple_of(start + SUB, SUB)

    def rows_of(order, comp, tile):
        return terms[order, comp, pl.ds(pl.multiple_of(base + tile * SUB, SUB), SUB), :]

    for comp in range(comps):
        smooth[comp, 0:SUB, :] = zero
        smooth[comp, SUB + rows:2 * SUB + rows, :] = zero
    for order in range(orders):
        for comp in range(comps):
            held = {}

            def along_y(tile):
                cells = rows_of(order, comp, tile)
                wide = cells + (left * pltpu.roll(cells, 1, 1) + right * pltpu.roll(cells, LANES - 1, 1))
                smooth[comp, SUB + tile * SUB:2 * SUB + tile * SUB, :] = wide
                held[tile] = (cells, wide)

            def along_x(tile):
                cells, wide = held.pop(tile)
                low = SUB + tile * SUB
                sides = smooth[comp, low - 1:low - 1 + SUB, :] + smooth[comp, low + 1:low + 1 + SUB, :]
                both = wide + 0.5 * sides
                if order == 0:
                    following = 0.5 * both - cells
                else:
                    following = (both - rows_of(order - 1, comp, tile)) - (cells + cells)
                terms[order + 1, comp, pl.ds(pl.multiple_of(base + tile * SUB, SUB), SUB), :] = following

            along_y(0)
            for tile in range(1, tiles):
                along_y(tile)
                along_x(tile - 1)
            along_x(tiles - 1)
    for tile in range(tiles):
        index = velocity_ref[layer, pl.ds(pl.multiple_of(start + tile * SUB, SUB), SUB), :]
        total = [None] * comps
        for order in range(orders + 1):
            parts = []
            for part in range(2):
                row = table_ref[pl.ds(table_row + 2 * order + part, 1), :]
                parts.append(jnp.take_along_axis(jnp.broadcast_to(row, (SUB, LANES)), index, axis=1, mode="promise_in_bounds"))
            re, im = parts
            cells = [rows_of(order, comp, tile) for comp in range(comps)]
            pieces = [re * cells[0] - im * cells[1], re * cells[1] + im * cells[0],
                      re * cells[2] + im * cells[3], re * cells[3] - im * cells[2]]
            total = [piece if old is None else old + piece for old, piece in zip(total, pieces)]
        for comp in range(comps):
            terms[0, comp, pl.ds(pl.multiple_of(base + tile * SUB, SUB), SUB), :] = total[comp]


def lane_weights():
    lane = lax.broadcasted_iota(jnp.int32, (SUB, LANES), 1)
    left = jnp.where(lane == 0, 0.0, 0.5).astype(jnp.float32)
    right = jnp.where(lane == LANES - 1, 0.0, 0.5).astype(jnp.float32)
    return left, right


def clear_edges(terms, domain):
    zero = jnp.zeros((SUB, LANES), jnp.float32)
    for comp in range(terms.shape[1]):
        terms[0, comp, 0:SUB, :] = zero
        terms[0, comp, SUB + domain:2 * SUB + domain, :] = zero


def run_layers(terms, smooth, table_ref, table_row, velocity_ref, shown_ref, own, width, reaches, domain):
    orders = terms.shape[0] - 1
    left, right = lane_weights()
    for layer, reach in enumerate(reaches):
        rows = min(domain, width + 2 * reach)
        start = jnp.minimum(jnp.maximum(own - reach, 0), domain - rows)
        start = pl.multiple_of(start, SUB)
        layer_step(terms, smooth, table_ref, table_row, velocity_ref, layer, start, rows, orders, None, left, right)
        for comp in range(terms.shape[1]):
            shown_ref[layer, comp] = terms[0, comp, pl.ds(pl.multiple_of(own, SUB), width + 2 * SUB), :]


def first_kernel(plan, table_ref, spot_ref, *refs):
    pieces, (field_ref, shown_ref, velocity_ref, terms, smooth) = refs[:plan.count], refs[plan.count:]
    clear_edges(terms, plan.domain)
    for number, piece in enumerate(pieces):
        at = pl.multiple_of(spot_ref[number] * plan.width, SUB)
        for comp in range(4):
            terms[0, comp, pl.ds(at + SUB, plan.width), :] = piece[comp]
        for layer in range(plan.layers):
            velocity_ref[layer, pl.ds(at, plan.width), :] = piece[4 + layer].astype(jnp.int32)
    own = spot_ref[plan.count] * plan.width
    run_layers(terms, smooth, table_ref, spot_ref[plan.count + 1], velocity_ref, shown_ref, own, plan.width,
               plan.reaches[0], plan.domain)
    for comp in range(4):
        field_ref[comp] = terms[0, comp, SUB:SUB + plan.domain, :]


def later_kernel(plan, tick, table_ref, spot_ref, velocity_ref, before_ref, *refs):
    pieces, (field_ref, shown_ref, terms, smooth) = refs[:plan.count], refs[plan.count:]
    clear_edges(terms, plan.domain)
    enters = spot_ref[plan.count + 2] == tick

    @pl.when(jnp.logical_not(enters))
    def _():
        for comp in range(4):
            terms[0, comp, SUB:SUB + plan.domain, :] = before_ref[comp]

    @pl.when(enters)
    def _():
        for number, piece in enumerate(pieces):
            at = pl.multiple_of(spot_ref[number] * plan.width, SUB)
            for comp in range(4):
                terms[0, comp, pl.ds(at + SUB, plan.width), :] = piece[comp]

    own = spot_ref[plan.count] * plan.width
    entered = spot_ref[plan.count + 2] <= tick
    table_row = jnp.where(entered, spot_ref[plan.count + 3], spot_ref[plan.count + 4])
    run_layers(terms, smooth, table_ref, table_row, velocity_ref, shown_ref, own, plan.width,
               plan.reaches[tick], plan.domain)
    if tick + 1 < plan.ticks:
        for comp in range(4):
            field_ref[comp] = terms[0, comp, SUB:SUB + plan.domain, :]
    else:
        for comp in range(4):
            field_ref[comp] = terms[0, comp, pl.ds(pl.multiple_of(own + SUB, SUB), plan.width), :]


def image_kernel(plan, count, has_base, offsets_ref, *refs):
    shown = refs[:count]
    base_ref = refs[count] if has_base else None
    image_ref = refs[-1]
    tiles = plan.width // SUB

    def one(index, carry):
        offset = offsets_ref[index]
        for layer in range(plan.layers):
            for tile in range(tiles):
                at = SUB + tile * SUB
                total = base_ref[layer, index, at - SUB:at, :] if has_base else None
                for ref in shown:
                    for part in range(2):
                        term = (ref[layer, part, pl.ds(at - offset, SUB), :]
                                * ref[layer, 2 + part, pl.ds(at + offset, SUB), :])
                        total = term if total is None else total + term
                image_ref[layer, index, at - SUB:at, :] = total
        return carry

    lax.fori_loop(0, offsets_ref.shape[0], one, 0)


class Plan:
    pass


def gathered(value, plan):
    if plan.everything:
        return [value] + [
            lax.ppermute(value, "strip", [(i, i ^ other) for i in range(plan.strips)])
            for other in range(1, plan.strips)
        ]
    whole = lax.all_gather(value, "strip")
    return [lax.dynamic_index_in_dim(whole, plan.first + number, 0, keepdims=False) for number in range(plan.count)]


def shifted(value, steps):
    count = lax.axis_size("depth")
    return lax.ppermute(value, "depth", [(i, (i + steps) % count) for i in range(count)])


def per_device(arrivals, feed, velocity_index, offsets, coef_table):
    plan = Plan()
    field = arrivals[0, 0]
    plan.width = field.shape[1]
    plan.layers = velocity_index.shape[0]
    plan.ticks = feed.shape[0] + 1
    plan.strips = lax.axis_size("strip")
    orders = coef_table.shape[1] - 1
    sections = lax.axis_size("depth")
    section = lax.axis_index("depth")
    strip = lax.axis_index("strip")
    last = plan.ticks - 1
    steps = plan.ticks * plan.layers
    side = -(-(orders * steps + SUB) // plan.width)
    plan.count = min(plan.strips, 2 * side + 1)
    plan.domain = plan.count * plan.width
    plan.everything = plan.count == plan.strips and plan.strips & (plan.strips - 1) == 0
    plan.first = jnp.clip(strip - side, 0, plan.strips - plan.count)
    plan.reaches = [
        [orders * (steps - tick * plan.layers - layer) + SUB for layer in range(plan.layers)]
        for tick in range(plan.ticks)
    ]
    size = coef_table.shape[1] * 2
    table = coef_table.reshape(coef_table.shape[0] * size, coef_table.shape[-1])
    table = jnp.pad(table, ((0, -table.shape[0] % SUB), (0, LANES - table.shape[1])))
    if plan.everything:
        places = jnp.arange(plan.count, dtype=jnp.int32) ^ strip
    else:
        places = jnp.arange(plan.count, dtype=jnp.int32)
    batch = sections - 1 + last - section
    extra = [strip - plan.first, (sections - 1 - section) * size, last - section,
             jnp.maximum(batch, 0) * size, jnp.maximum(batch - sections, 0) * size]
    lane = jnp.arange(len(extra), dtype=jnp.int32)
    tail = sum(jnp.where(lane == number, value, 0) for number, value in enumerate(extra))
    spots = jnp.concatenate([places, tail.astype(jnp.int32)])

    message = jnp.concatenate([field, velocity_index.astype(jnp.float32)], axis=0)
    pieces = gathered(message, plan)

    full = jax.ShapeDtypeStruct((4, plan.domain, LANES), jnp.float32)
    shown = jax.ShapeDtypeStruct((plan.layers, 4, plan.width + 2 * SUB, LANES), jnp.float32)
    levels = jax.ShapeDtypeStruct((plan.layers, plan.domain, LANES), jnp.int32)
    scratch = [pltpu.VMEM((orders + 1, 4, plan.domain + 2 * SUB, LANES), jnp.float32),
               pltpu.VMEM((4, plan.domain + 2 * SUB, LANES), jnp.float32)]
    cost = pl.CostEstimate(flops=100_000_000, bytes_accessed=4_000_000, transcendentals=0)
    field, shown_first, velocity = pl.pallas_call(
        functools.partial(first_kernel, plan),
        out_shape=(full, shown, levels),
        in_specs=[VMEM, SMEM] + [VMEM] * plan.count,
        out_specs=(VMEM,) * 3,
        scratch_shapes=scratch,
        cost_estimate=cost,
        name="first",
    )(table, spots, *pieces)
    moved = shifted(field, last)
    velocities = [shifted(velocity, last - tick) if tick < last else velocity for tick in range(1, plan.ticks)]
    own_feed = lax.dynamic_index_in_dim(feed, jnp.clip(last - 1 - section, 0, last - 1), 0, keepdims=False)[0]
    feeds = gathered(own_feed, plan)

    def imaged(parts, base):
        image = jax.ShapeDtypeStruct((plan.layers, offsets.shape[0], plan.width, LANES), jnp.float32)
        extra = () if base is None else (base,)
        return pl.pallas_call(
            functools.partial(image_kernel, plan, len(parts), base is not None),
            out_shape=image,
            in_specs=[SMEM] + [VMEM] * (len(parts) + len(extra)),
            out_specs=VMEM,
            cost_estimate=pl.CostEstimate(flops=10_000_000, bytes_accessed=2_000_000, transcendentals=0),
            name="image",
        )(offsets, *parts, *extra)

    image = imaged([shown_first], None)
    parts = []
    for tick in range(1, plan.ticks):
        out = full if tick < last else jax.ShapeDtypeStruct((4, plan.width, LANES), jnp.float32)
        moved, seen = pl.pallas_call(
            functools.partial(later_kernel, plan, tick),
            out_shape=(out, shown),
            in_specs=[VMEM, SMEM, VMEM, VMEM] + [VMEM] * plan.count,
            out_specs=(VMEM,) * 2,
            scratch_shapes=scratch,
            cost_estimate=cost,
            name=f"later{tick}",
        )(table, spots, velocities[tick - 1], moved, *feeds)
        parts.append(seen if tick == last else shifted(seen, tick - last))
    image = imaged(parts, image)
    return image, moved[None, None]


def solution(mesh):
    placed = (
        P("depth", None, None, "strip", None),
        P(None, None, None, "strip", None),
        P("depth", "strip", None),
        P(),
        P(),
    )
    return jax.shard_map(
        per_device,
        mesh=mesh,
        in_specs=placed,
        out_specs=(P("depth", None, "strip", None), P("depth", None, None, "strip", None)),
        check_vma=False,
    )
```

time: 180 us -> 58.6 us (0.33)
  the two profiles are of different devices: /device:TPU:28 before, /device:TPU:1 now
where the time goes in v1:
time: 58.6 us; the launch traced here: 58.3 us
  Pallas kernels  25.6 us (44%)
  starting transfers between devices  13.3 us (23%)
  waiting for transfers between devices  10.9 us (19%)
  local copies, waits for them, and re-layouts  5.33 us (9%)
  other arithmetic  2.41 us (4%)
  between operations  0.76 us (1%)
    pallas_call x3, Pallas kernels, per_device(): pl.pallas_call(functools.partial(later_kernel, plan, tick), out_shape=(ou...  15.1 us
    ppermute x6, waiting for transfers between devices, gathered(): lax.ppermute(value, 'strip', [(i, i ^ other) for i in range(plan.strips)])  10.9 us
    ppermute x6, starting transfers between devices, gathered(): lax.ppermute(value, 'strip', [(i, i ^ other) for i in range(plan.strips)])  7.18 us
    ppermute x5, starting transfers between devices, shifted(): lax.ppermute(value, 'depth', [(i, (i + steps) % count) for i in range(cou...  6.14 us
    pallas_call x1, Pallas kernels, per_device(): pl.pallas_call(functools.partial(first_kernel, plan), out_shape=(full, sh...  5.79 us
    pallas_call x2, Pallas kernels, imaged(): pl.pallas_call(functools.partial(image_kernel, plan, len(parts), base is...  4.68 us
    unnamed x35, local copies, waits for them, and re-layouts  4.59 us
  transfers between devices with their start and end apart: 11, of which 4 were waited for; matrix products, arithmetic and copies ran while one was open for 5% of the time, Pallas kernels for 29%

profile of v1, /device:TPU:1, one launch (start us, length us, event | category | flops | bytes accessed | tf_op | source)
XLA Modules:
  0.0 58.3 jit_solution(13198980313843182145)
XLA Ops:
  0.7 0.8 %convert_element_type.5 = f32[2,32,128]{2,1,0:T(8,128)S(1)} convert(s32[2,32,128]{2,1,0:T(8,128)} %param.7) | non-fusion elementwise | flops 8192 | bytes 65536 | tf_op jit(solution)/shard_map/convert_element_type | solution.py:221
  1.6 4.2 %collective-permute-start.2 = (f32[6,32,128]{2,1,0:T(8,128)S(1)}, f32[6,32,128]{2,1,0:T(8,128)S(1)}, u32[]{:S(2)}, u32[]{:S(2)}) collective-permute-start(f32[6,32,128]{2,1,0:T(8,128)S(1)} %pad_maximum_fusion.refs_0_), channel_id=1, source_target_pairs={{0,3},{1,2},{2,1},{3,0},{4,7},{5,6},{6,5},{7,4},{8,11},{9,10},{10,... | collective-permute-start | bytes 294920 | tf_op jit(solution)/shard_map/ppermute | solution.py:173
  6.6 1.0 %reduce.3 = f32[11,9,2,32]{3,2,1,0:T(2,128)S(1)} reduce(f32[11,9,2,1,32]{4,3,2,1,0:T(1,128)S(1)} %copy-done.12, f32[]{:T(128)} %broadcast.30), dimensions={3}, to_apply=%param.9.reduce_sub_computation.3 | reduce | bytes 50692 | tf_op args[4]
  7.7 0.7 %pad.4.table_ref = f32[200,128]{1,0:T(8,128)} pad(f32[198,32]{1,0:T(8,128)S(1)} %reshape.8, f32[]{:T(128)} %constant.13.clone.1), padding=0_2x0_96 | pad | bytes 127748 | tf_op jit(solution)/shard_map/jit(_pad)/pad | solution.py:209
  9.0 4.7 %collective-permute-done.1.refs_2_ = f32[6,32,128]{2,1,0:T(8,128)S(1)} collective-permute-done((f32[6,32,128]{2,1,0:T(8,128)S(1)}, f32[6,32,128]{2,1,0:T(8,128)S(1)}, u32[]{:S(2)}, u32[]{:S(2)}) %collective-permute-start.1) | collective-permute-done | bytes 98336 | tf_op jit(solution)/shard_map/ppermute | solution.py:173
  13.7 0.6 %copy-done.14 = f32[6,32,128]{2,1,0:T(8,128)} copy-done((f32[6,32,128]{2,1,0:T(8,128)}, f32[6,32,128]{2,1,0:T(8,128)S(1)}, u32[]{:S(2)}) %copy-start.14) | copy-done | bytes 98328
  14.3 0.6 %copy-done.15 = f32[6,32,128]{2,1,0:T(8,128)} copy-done((f32[6,32,128]{2,1,0:T(8,128)}, f32[6,32,128]{2,1,0:T(8,128)S(1)}, u32[]{:S(2)}) %copy-start.15) | copy-done | bytes 98328
  14.9 5.8 %first.1 = (f32[4,128,128]{2,1,0:T(8,128)}, f32[2,4,48,128]{3,2,1,0:T(8,128)}, s32[2,128,128]{2,1,0:T(8,128)}) custom-call(f32[200,128]{1,0:T(8,128)} %pad.4.table_ref, s32[9]{0:T(128)} %pad_add_fusion.spot_ref, f32[6,32,128]{2,1,0:T(8,128)} %copy-done.5, f32[6,32,128]{2,1,0:T(8,128)} %copy-done.15, f32[6,32,128]{2,1,0:T(8,128)} %copy-done.14, ...), custom_call_target="tpu_custom_call" | custom-call | flops 100000000 | bytes 4000000 | tf_op jit(solution)/shard_map/first/pallas_call | solution.py:230
  20.7 2.5 %collective-permute-start.4 = (f32[4,128,128]{2,1,0:T(8,128)}, f32[4,128,128]{2,1,0:T(8,128)S(1)}, u32[]{:S(2)}, u32[]{:S(2)}) collective-permute-start(f32[4,128,128]{2,1,0:T(8,128)} %get-tuple-element.12), channel_id=1, source_target_pairs={{0,12},{4,16},{8,20},{12,24},{16,28},{20,0},{24,4},{28,8},{1,13},{... | collective-permute-start | bytes 786440 | tf_op jit(solution)/shard_map/ppermute | solution.py:182
  23.2 2.3 %collective-permute-start.7 = (f32[4,32,128]{2,1,0:T(8,128)S(1)}, f32[4,32,128]{2,1,0:T(8,128)S(1)}, u32[]{:S(2)}, u32[]{:S(2)}) collective-permute-start(f32[4,32,128]{2,1,0:T(8,128)S(1)} %dynamic-slice_bitcast_fusion.refs_0_), channel_id=1, source_target_pairs={{0,3},{1,2},{2,1},{3,0},{4,7},{5,6},{6,5},{7,4},{8,11},{9,10},{10,... | collective-permute-start | bytes 196616 | tf_op jit(solution)/shard_map/ppermute | solution.py:173
  25.5 1.2 %collective-permute-start.3 = (s32[2,128,128]{2,1,0:T(8,128)S(1)}, s32[2,128,128]{2,1,0:T(8,128)S(1)}, u32[]{:S(2)}, u32[]{:S(2)}) collective-permute-start(s32[2,128,128]{2,1,0:T(8,128)S(1)} %copy-done.9), channel_id=1, source_target_pairs={{0,8},{4,12},{8,16},{12,20},{16,24},{20,28},{24,0},{28,4},{1,9},{5... | collective-permute-start | bytes 393224 | tf_op jit(solution)/shard_map/ppermute | solution.py:182
  27.3 1.2 %collective-permute-done.7.refs_3_ = f32[4,32,128]{2,1,0:T(8,128)S(1)} collective-permute-done((f32[4,32,128]{2,1,0:T(8,128)S(1)}, f32[4,32,128]{2,1,0:T(8,128)S(1)}, u32[]{:S(2)}, u32[]{:S(2)}) %collective-permute-start.7) | collective-permute-done | bytes 65568 | tf_op jit(solution)/shard_map/ppermute | solution.py:173
  28.8 3.5 %collective-permute-done.6.refs_2_ = f32[4,32,128]{2,1,0:T(8,128)S(1)} collective-permute-done((f32[4,32,128]{2,1,0:T(8,128)S(1)}, f32[4,32,128]{2,1,0:T(8,128)S(1)}, u32[]{:S(2)}, u32[]{:S(2)}) %collective-permute-start.6) | collective-permute-done | bytes 65568 | tf_op jit(solution)/shard_map/ppermute | solution.py:173
  32.3 1.5 %collective-permute-done.5.refs_1_ = f32[4,32,128]{2,1,0:T(8,128)S(1)} collective-permute-done((f32[4,32,128]{2,1,0:T(8,128)S(1)}, f32[4,32,128]{2,1,0:T(8,128)S(1)}, u32[]{:S(2)}, u32[]{:S(2)}) %collective-permute-start.5) | collective-permute-done | bytes 65568 | tf_op jit(solution)/shard_map/ppermute | solution.py:173
  34.5 0.7 %copy-done.6 = f32[4,128,128]{2,1,0:T(8,128)} copy-done((f32[4,128,128]{2,1,0:T(8,128)}, f32[4,128,128]{2,1,0:T(8,128)S(1)}, u32[]{:S(2)}) %copy-start.6) | copy-done | bytes 262168
  35.2 5.8 %later1.1 = (f32[4,128,128]{2,1,0:T(8,128)}, f32[2,4,48,128]{3,2,1,0:T(8,128)}) custom-call(f32[200,128]{1,0:T(8,128)} %pad.4.table_ref, s32[9]{0:T(128)} %pad_add_fusion.spot_ref, s32[2,128,128]{2,1,0:T(8,128)} %copy-done.11, f32[4,128,128]{2,1,0:T(8,128)} %copy-done.6, f32[4,32,128]{2,1,0:T(8,128)} %copy-done.1, f32[4,32,128]{2,1,0:T(8,128)} %copy-done.4, ...), custom_call_target="tpu_custom_call" | custom-call | flops 100000000 | bytes 4000000 | tf_op jit(solution)/shard_map/later1/pallas_call | solution.py:260
  41.0 1.0 %collective-permute-start.8 = (f32[2,4,48,128]{3,2,1,0:T(8,128)}, f32[2,4,48,128]{3,2,1,0:T(8,128)S(1)}, u32[]{:S(2)}, u32[]{:S(2)}) collective-permute-start(f32[2,4,48,128]{3,2,1,0:T(8,128)} %get-tuple-element.13), channel_id=1, source_target_pairs={{0,24},{4,28},{8,0},{12,4},{16,8},{20,12},{24,16},{28,20},{1,25},{... | collective-permute-start | bytes 589832 | tf_op jit(solution)/shard_map/ppermute | solution.py:182
  41.9 0.6 %copy-done.10 = s32[2,128,128]{2,1,0:T(8,128)} copy-done((s32[2,128,128]{2,1,0:T(8,128)}, s32[2,128,128]{2,1,0:T(8,128)S(1)}, u32[]{:S(2)}) %copy-start.10) | copy-done | bytes 131096
  42.6 5.1 %later2.1 = (f32[4,128,128]{2,1,0:T(8,128)}, f32[2,4,48,128]{3,2,1,0:T(8,128)}) custom-call(f32[200,128]{1,0:T(8,128)} %pad.4.table_ref, s32[9]{0:T(128)} %pad_add_fusion.spot_ref, s32[2,128,128]{2,1,0:T(8,128)} %copy-done.10, f32[4,128,128]{2,1,0:T(8,128)} %get-tuple-element.14.before_ref, f32[4,32,128]{2,1,0:T(8,128)} %copy-done.1, ...), custom_call_target="tpu_custom_call" | custom-call | flops 100000000 | bytes 4000000 | tf_op jit(solution)/shard_map/later2/pallas_call | solution.py:260
  47.7 0.9 %collective-permute-start.10 = (f32[2,4,48,128]{3,2,1,0:T(8,128)}, f32[2,4,48,128]{3,2,1,0:T(8,128)S(1)}, u32[]{:S(2)}, u32[]{:S(2)}) collective-permute-start(f32[2,4,48,128]{3,2,1,0:T(8,128)} %get-tuple-element.15), channel_id=1, source_target_pairs={{0,28},{4,0},{8,4},{12,8},{16,12},{20,16},{24,20},{28,24},{1,29},{... | collective-permute-start | bytes 589832 | tf_op jit(solution)/shard_map/ppermute | solution.py:182
  48.6 2.0 %image.2.refs_3_ = f32[2,16,32,128]{3,2,1,0:T(8,128)} custom-call(s32[16]{0:T(128)} %offsets_ref.3, f32[2,4,48,128]{3,2,1,0:T(8,128)} %get-tuple-element.18.refs_0_), custom_call_target="tpu_custom_call" | custom-call | flops 10000000 | bytes 2000000 | tf_op jit(solution)/shard_map/image/pallas_call | solution.py:247
  50.6 4.2 %later3.1 = (f32[4,32,128]{2,1,0:T(8,128)}, f32[2,4,48,128]{3,2,1,0:T(8,128)}) custom-call(f32[200,128]{1,0:T(8,128)} %pad.4.table_ref, s32[9]{0:T(128)} %pad_add_fusion.spot_ref, s32[2,128,128]{2,1,0:T(8,128)} %get-tuple-element.11.velocity_ref, f32[4,128,128]{2,1,0:T(8,128)} %get-tuple-element.16.before_ref, f32[4,32,128]{2,1,0:T(8,128)} %copy-done.1, ...), custom_call_target="tpu_custom_call" | custom-call | flops 100000000 | bytes 4000000 | tf_op jit(solution)/shard_map/later3/pallas_call | solution.py:260
  54.9 0.6 %copy-done.7 = f32[2,4,48,128]{3,2,1,0:T(8,128)} copy-done((f32[2,4,48,128]{3,2,1,0:T(8,128)}, f32[2,4,48,128]{3,2,1,0:T(8,128)S(1)}, u32[]{:S(2)}) %copy-start.7) | copy-done | bytes 196632
  55.6 2.7 %image.3 = f32[2,16,32,128]{3,2,1,0:T(8,128)} custom-call(s32[16]{0:T(128)} %offsets_ref.3, f32[2,4,48,128]{3,2,1,0:T(8,128)} %copy-done.7, f32[2,4,48,128]{3,2,1,0:T(8,128)} %copy-done.8, f32[2,4,48,128]{3,2,1,0:T(8,128)} %get-tuple-element.17.refs_2_, f32[2,16,32,128]{3,2,1,0:T(8,128)} %image.2.refs_3_), custom_call_target="tpu_custom_call" | custom-call | flops 10000000 | bytes 2000000 | tf_op jit(solution)/shard_map/image/pallas_call | solution.py:247
  (48 shorter events, 3.3 us)
Async XLA Ops:
  0.6 22.5 %copy-start = (f32[3,1,4,32,128]{4,3,2,1,0:T(8,128)S(1)}, f32[3,1,4,32,128]{4,3,2,1,0:T(8,128)}, u32[]{:S(2)}) copy-start(f32[3,1,4,32,128]{4,3,2,1,0:T(8,128)} %param.6) | copy-start | bytes 589828
  0.6 0.9 %copy-start.16 = (f32[1,1,4,32,128]{4,3,2,1,0:T(8,128)S(1)}, f32[1,1,4,32,128]{4,3,2,1,0:T(8,128)}, u32[]{:S(2)}) copy-start(f32[1,1,4,32,128]{4,3,2,1,0:T(8,128)} %param.5) | copy-start | bytes 196612
  1.5 5.1 %copy-start.12 = (f32[11,9,2,1,32]{4,3,2,1,0:T(1,128)S(1)}, f32[11,9,2,1,32]{4,3,2,1,0:T(1,128)}, u32[]{:S(2)}) copy-start(f32[11,9,2,1,32]{4,3,2,1,0:T(1,128)} %param.9) | copy-start | bytes 76036
  1.6 6.1 %copy-start.5 = (f32[6,32,128]{2,1,0:T(8,128)}, f32[6,32,128]{2,1,0:T(8,128)S(1)}, u32[]{:S(2)}) copy-start(f32[6,32,128]{2,1,0:T(8,128)S(1)} %pad_maximum_fusion.refs_0_) | copy-start | bytes 294916
  1.6 7.4 %collective-permute-start.2 = (f32[6,32,128]{2,1,0:T(8,128)S(1)}, f32[6,32,128]{2,1,0:T(8,128)S(1)}, u32[]{:S(2)}, u32[]{:S(2)}) collective-permute-start(f32[6,32,128]{2,1,0:T(8,128)S(1)} %pad_maximum_fusion.refs_0_), channel_id=1, source_target_pairs={{0,3},{1,2},{2,1},{3,0},{4,7},{5,6},{6,5},{7,4},{8,11},{9,10},{10,... | collective-permute-start | bytes 294920 | tf_op jit(solution)/shard_map/ppermute | solution.py:173
  5.8 7.9 %collective-permute-start.1 = (f32[6,32,128]{2,1,0:T(8,128)S(1)}, f32[6,32,128]{2,1,0:T(8,128)S(1)}, u32[]{:S(2)}, u32[]{:S(2)}) collective-permute-start(f32[6,32,128]{2,1,0:T(8,128)S(1)} %pad_maximum_fusion.refs_0_), channel_id=1, source_target_pairs={{0,2},{1,3},{2,0},{3,1},{4,6},{5,7},{6,4},{7,5},{8,10},{9,11},{10,... | collective-permute-start | bytes 294920 | tf_op jit(solution)/shard_map/ppermute | solution.py:173
  5.8 7.9 %collective-permute-start = (f32[6,32,128]{2,1,0:T(8,128)S(1)}, f32[6,32,128]{2,1,0:T(8,128)S(1)}, u32[]{:S(2)}, u32[]{:S(2)}) collective-permute-start(f32[6,32,128]{2,1,0:T(8,128)S(1)} %pad_maximum_fusion.refs_0_), channel_id=1, source_target_pairs={{0,1},{1,0},{2,3},{3,2},{4,5},{5,4},{6,7},{7,6},{8,9},{9,8},{10,11... | collective-permute-start | bytes 294920 | tf_op jit(solution)/shard_map/ppermute | solution.py:173
  9.0 4.7 %copy-start.13 = (f32[6,32,128]{2,1,0:T(8,128)}, f32[6,32,128]{2,1,0:T(8,128)S(1)}, u32[]{:S(2)}) copy-start(f32[6,32,128]{2,1,0:T(8,128)S(1)} %collective-permute-done.2.refs_3_) | copy-start | bytes 294916
  20.7 4.8 %copy-start.9 = (s32[2,128,128]{2,1,0:T(8,128)S(1)}, s32[2,128,128]{2,1,0:T(8,128)}, u32[]{:S(2)}) copy-start(s32[2,128,128]{2,1,0:T(8,128)} %get-tuple-element.11.velocity_ref) | copy-start | bytes 393220
  20.7 13.1 %collective-permute-start.4 = (f32[4,128,128]{2,1,0:T(8,128)}, f32[4,128,128]{2,1,0:T(8,128)S(1)}, u32[]{:S(2)}, u32[]{:S(2)}) collective-permute-start(f32[4,128,128]{2,1,0:T(8,128)} %get-tuple-element.12), channel_id=1, source_target_pairs={{0,12},{4,16},{8,20},{12,24},{16,28},{20,0},{24,4},{28,8},{1,13},{... | collective-permute-start | bytes 786440 | tf_op jit(solution)/shard_map/ppermute | solution.py:182
  23.2 10.6 %copy-start.1 = (f32[4,32,128]{2,1,0:T(8,128)}, f32[4,32,128]{2,1,0:T(8,128)S(1)}, u32[]{:S(2)}) copy-start(f32[4,32,128]{2,1,0:T(8,128)S(1)} %dynamic-slice_bitcast_fusion.refs_0_) | copy-start | bytes 196612
  23.2 5.3 %collective-permute-start.7 = (f32[4,32,128]{2,1,0:T(8,128)S(1)}, f32[4,32,128]{2,1,0:T(8,128)S(1)}, u32[]{:S(2)}, u32[]{:S(2)}) collective-permute-start(f32[4,32,128]{2,1,0:T(8,128)S(1)} %dynamic-slice_bitcast_fusion.refs_0_), channel_id=1, source_target_pairs={{0,3},{1,2},{2,1},{3,0},{4,7},{5,6},{6,5},{7,4},{8,11},{9,10},{10,... | collective-permute-start | bytes 196616 | tf_op jit(solution)/shard_map/ppermute | solution.py:173
  25.5 8.3 %collective-permute-start.3 = (s32[2,128,128]{2,1,0:T(8,128)S(1)}, s32[2,128,128]{2,1,0:T(8,128)S(1)}, u32[]{:S(2)}, u32[]{:S(2)}) collective-permute-start(s32[2,128,128]{2,1,0:T(8,128)S(1)} %copy-done.9), channel_id=1, source_target_pairs={{0,8},{4,12},{8,16},{12,20},{16,24},{20,28},{24,0},{28,4},{1,9},{5... | collective-permute-start | bytes 393224 | tf_op jit(solution)/shard_map/ppermute | solution.py:182
  26.7 15.2 %collective-permute-start.9 = (s32[2,128,128]{2,1,0:T(8,128)S(1)}, s32[2,128,128]{2,1,0:T(8,128)S(1)}, u32[]{:S(2)}, u32[]{:S(2)}) collective-permute-start(s32[2,128,128]{2,1,0:T(8,128)S(1)} %copy-done.9), channel_id=1, source_target_pairs={{0,4},{4,8},{8,12},{12,16},{16,20},{20,24},{24,28},{28,0},{1,5},{5... | collective-permute-start | bytes 393224 | tf_op jit(solution)/shard_map/ppermute | solution.py:182
  27.3 5.0 %collective-permute-start.6 = (f32[4,32,128]{2,1,0:T(8,128)S(1)}, f32[4,32,128]{2,1,0:T(8,128)S(1)}, u32[]{:S(2)}, u32[]{:S(2)}) collective-permute-start(f32[4,32,128]{2,1,0:T(8,128)S(1)} %dynamic-slice_bitcast_fusion.refs_0_), channel_id=1, source_target_pairs={{0,2},{1,3},{2,0},{3,1},{4,6},{5,7},{6,4},{7,5},{8,10},{9,11},{10,... | collective-permute-start | bytes 196616 | tf_op jit(solution)/shard_map/ppermute | solution.py:173
  28.5 5.4 %copy-start.2 = (f32[4,32,128]{2,1,0:T(8,128)}, f32[4,32,128]{2,1,0:T(8,128)S(1)}, u32[]{:S(2)}) copy-start(f32[4,32,128]{2,1,0:T(8,128)S(1)} %collective-permute-done.7.refs_3_) | copy-start | bytes 196612
  28.5 5.3 %collective-permute-start.5 = (f32[4,32,128]{2,1,0:T(8,128)S(1)}, f32[4,32,128]{2,1,0:T(8,128)S(1)}, u32[]{:S(2)}, u32[]{:S(2)}) collective-permute-start(f32[4,32,128]{2,1,0:T(8,128)S(1)} %dynamic-slice_bitcast_fusion.refs_0_), channel_id=1, source_target_pairs={{0,1},{1,0},{2,3},{3,2},{4,5},{5,4},{6,7},{7,6},{8,9},{9,8},{10,11... | collective-permute-start | bytes 196616 | tf_op jit(solution)/shard_map/ppermute | solution.py:173
  32.3 1.6 %copy-start.3 = (f32[4,32,128]{2,1,0:T(8,128)}, f32[4,32,128]{2,1,0:T(8,128)S(1)}, u32[]{:S(2)}) copy-start(f32[4,32,128]{2,1,0:T(8,128)S(1)} %collective-permute-done.6.refs_2_) | copy-start | bytes 196612
  33.8 0.7 %copy-start.11 = (s32[2,128,128]{2,1,0:T(8,128)}, s32[2,128,128]{2,1,0:T(8,128)S(1)}, u32[]{:S(2)}) copy-start(s32[2,128,128]{2,1,0:T(8,128)S(1)} %collective-permute-done.3.velocity_ref) | copy-start | bytes 393220
  34.5 0.7 %copy-start.6 = (f32[4,128,128]{2,1,0:T(8,128)}, f32[4,128,128]{2,1,0:T(8,128)S(1)}, u32[]{:S(2)}) copy-start(f32[4,128,128]{2,1,0:T(8,128)S(1)} %collective-permute-done.4.before_ref) | copy-start | bytes 786436
  41.0 13.9 %collective-permute-start.8 = (f32[2,4,48,128]{3,2,1,0:T(8,128)}, f32[2,4,48,128]{3,2,1,0:T(8,128)S(1)}, u32[]{:S(2)}, u32[]{:S(2)}) collective-permute-start(f32[2,4,48,128]{3,2,1,0:T(8,128)} %get-tuple-element.13), channel_id=1, source_target_pairs={{0,24},{4,28},{8,0},{12,4},{16,8},{20,12},{24,16},{28,20},{1,25},{... | collective-permute-start | bytes 589832 | tf_op jit(solution)/shard_map/ppermute | solution.py:182
  47.7 7.1 %collective-permute-start.10 = (f32[2,4,48,128]{3,2,1,0:T(8,128)}, f32[2,4,48,128]{3,2,1,0:T(8,128)S(1)}, u32[]{:S(2)}, u32[]{:S(2)}) collective-permute-start(f32[2,4,48,128]{3,2,1,0:T(8,128)} %get-tuple-element.15), channel_id=1, source_target_pairs={{0,28},{4,0},{8,4},{12,8},{16,12},{20,16},{24,20},{28,24},{1,29},{... | collective-permute-start | bytes 589832 | tf_op jit(solution)/shard_map/ppermute | solution.py:182
  54.8 0.7 %copy-start.7 = (f32[2,4,48,128]{3,2,1,0:T(8,128)}, f32[2,4,48,128]{3,2,1,0:T(8,128)S(1)}, u32[]{:S(2)}) copy-start(f32[2,4,48,128]{3,2,1,0:T(8,128)S(1)} %collective-permute-done.8.refs_0_) | copy-start | bytes 589828
  54.9 0.7 %copy-start.8 = (f32[2,4,48,128]{3,2,1,0:T(8,128)}, f32[2,4,48,128]{3,2,1,0:T(8,128)S(1)}, u32[]{:S(2)}) copy-start(f32[2,4,48,128]{3,2,1,0:T(8,128)S(1)} %collective-permute-done.10.refs_1_) | copy-start | bytes 589828
  (4 other events, 2.5 us)
